TPU v7x, 128 devices: a whole 4x4x4 slice. The times are simulated.
128 devices in a mesh: gx: 16 (over z, x_hi, core), gy: 8 (over x_lo, y).
Axes of the slice: x: 4 (x_hi: 2, x_lo: 2; x = x_hi * 2 + x_lo), y: 4, z: 4, core: 2. Of those that a mesh axis runs over, the one named last changes fastest.
Arguments:
- grid_field: bfloat16 [1, 20, 2048, 2048], P(None, None, 'gx', 'gy'), may hold values from -8 to 8
- spectral_weight: float32 [2, 2, 20, 20, 2048], P(None, None, None, None, ('gx', 'gy')), may hold values from -1 to 1
- conv_near: bfloat16 [2, 20, 180], replicated, may hold values from -0.4375 to 0.4375
- conv_far: bfloat16 [2, 20, 500], replicated, may hold values from -0.25 to 0.25
- mix_logits: float32 [2, 3], replicated, may hold values from -1 to 1
- channel_bias: float32 [2, 20], replicated, may hold values from -3 to 3
Outputs:
- result_field: bfloat16 [1, 20, 2048, 2048], P(None, None, 'gx', 'gy')
All inputs are finite; a program needn't handle non-finite values.
Results may differ from a plain program's by a relative error of at most 0.004.
Values may be sent and summed in bfloat16 or wider, within the bound.
No kernel may reach another device: no remote copies, remote signals or barrier semaphores. Data moves between devices by JAX's collectives and lax.ppermute only.
A program may use at most 192 MiB of HBM per device.

v0:
```python
import math
import jax
import jax.numpy as jnp
from jax import lax
from jax.sharding import PartitionSpec as P

NX = 2048
NY = 2048
MX = 32
MY = 32
LAYERS = 2
KX = 64
MODES = 2048
full_turn = 2.0 * math.pi
highest = lax.Precision.HIGHEST


def padded_2(value, sides, width):
    for axis, dim in sides:
        size, length = (lax.axis_size(axis), value.shape[dim])
        up = [(i, (i + 1) % size) for i in range(size)]
        down = [(j, i) for i, j in up]
        last = lax.slice_in_dim(value, length - width, length, axis=dim)
        first = lax.slice_in_dim(value, 0, width, axis=dim)
        before = lax.ppermute(last, axis, up)
        after = lax.ppermute(first, axis, down)
        value = jnp.concatenate([before, value, after], axis=dim)
    return value


def forward_table(positions):
    col_modes = jnp.arange(MY, dtype=jnp.int32)
    phases = (positions[:, None] * col_modes[None, :] % NY).astype(jnp.float32) * (full_turn / NY)
    return jnp.concatenate([jnp.cos(phases), -jnp.sin(phases)], axis=1).astype(jnp.bfloat16)


def row_tables(positions):
    lower = jnp.arange(MX, dtype=jnp.int32)
    row_modes = jnp.concatenate([lower, lower + (NX - MX)])
    phases = (positions[:, None] * row_modes[None, :] % NX).astype(jnp.float32) * (full_turn / NX)
    return (jnp.cos(phases), jnp.sin(phases))


def inverse_table(positions):
    col_modes = jnp.arange(MY, dtype=jnp.int32)
    col_weight = jnp.where(col_modes == 0, 1.0, 2.0).astype(jnp.float32) / (NX * NY)
    phases = (col_modes[:, None] * positions[None, :] % NY).astype(jnp.float32) * (full_turn / NY)
    return jnp.concatenate(
        [jnp.cos(phases) * col_weight[:, None], -jnp.sin(phases) * col_weight[:, None]], axis=0
    )


def conv_rows(padded_plane, tap_weights, dilation, side_taps, first_row, count_rows, local_cols):
    channels = padded_plane.shape[0]
    pieces = []
    for row_tap in range(side_taps):
        for col_tap in range(side_taps):
            row_offset = 4 + (row_tap - side_taps // 2) * dilation + first_row
            col_offset = 4 + (col_tap - side_taps // 2) * dilation
            pieces.append(
                padded_plane[
                    :, row_offset : row_offset + count_rows, col_offset : col_offset + local_cols
                ]
            )
    stacked = jnp.stack(pieces, 0)
    shaped_weights = tap_weights.reshape(channels, side_taps * side_taps, channels)
    return jnp.einsum("otc,tcxy->oxy", shaped_weights, stacked, preferred_element_type=jnp.float32)


def on_device(grid_field, spectral_weight, conv_near, conv_far, mix_logits, channel_bias):
    channels = grid_field.shape[1]
    local_rows = grid_field.shape[2]
    local_cols = grid_field.shape[3]
    row_positions = lax.axis_index("gx") * local_rows + jnp.arange(local_rows, dtype=jnp.int32)
    col_positions = lax.axis_index("gy") * local_cols + jnp.arange(local_cols, dtype=jnp.int32)
    forward_cols = forward_table(col_positions)
    cosine_rows, sine_rows = row_tables(row_positions)
    inverse_cols = inverse_table(col_positions)
    share_modes = spectral_weight.shape[-1]
    owner_index = lax.axis_index("gx") * lax.axis_size("gy") + lax.axis_index("gy")
    mode_start = owner_index * share_modes
    row_blocks = max(1, local_rows // 32)
    while local_rows % row_blocks != 0:
        row_blocks = row_blocks - 1
    block_rows = local_rows // row_blocks
    planes_block = grid_field
    for layer_index in range(LAYERS):
        planes_here = planes_block.shape[0]
        line_sums = jnp.dot(
            planes_block.reshape(planes_here * channels * local_rows, local_cols),
            forward_cols,
            preferred_element_type=jnp.float32,
        )
        line_sums = line_sums.reshape(planes_here, channels, local_rows, 2 * MY)
        real_lines = line_sums[..., :MY]
        imaginary_lines = line_sums[..., MY:]

        def contract_rows(operand, lookup):
            return jnp.einsum("pcxk,xj->pcjk", operand, lookup, precision=highest)

        real_spec = contract_rows(real_lines, cosine_rows) + contract_rows(
            imaginary_lines, sine_rows
        )
        imaginary_spec = contract_rows(imaginary_lines, cosine_rows) - contract_rows(
            real_lines, sine_rows
        )
        partial_value = jnp.stack(
            [
                real_spec.reshape(planes_here, channels, MODES),
                imaginary_spec.reshape(planes_here, channels, MODES),
            ]
        )
        totals = lax.psum(partial_value, ("gx", "gy"))
        own_modes = lax.dynamic_slice_in_dim(totals, mode_start, share_modes, 3)

        def mix_modes(spectrum, weights):
            return jnp.einsum("pcm,com->pom", spectrum, weights, precision=highest)

        weight_real = spectral_weight[layer_index, 0]
        weight_imaginary = spectral_weight[layer_index, 1]
        real_mixed = mix_modes(own_modes[0], weight_real) - mix_modes(
            own_modes[1], weight_imaginary
        )
        imaginary_mixed = mix_modes(own_modes[1], weight_real) + mix_modes(
            own_modes[0], weight_imaginary
        )
        own_block = jnp.stack([real_mixed, imaginary_mixed])[None]
        gathered = lax.all_gather(own_block, ("gx", "gy"), axis=0, tiled=True)
        gathered = jnp.transpose(gathered, (1, 2, 3, 0, 4)).reshape(2, planes_here, channels, MODES)
        real_full = gathered[0].reshape(planes_here, channels, KX, MY)
        imaginary_full = gathered[1].reshape(planes_here, channels, KX, MY)

        def expand_rows(spectrum, lookup):
            return jnp.einsum("pcjk,xj->pcxk", spectrum, lookup, precision=highest)

        real_rows = expand_rows(real_full, cosine_rows) - expand_rows(imaginary_full, sine_rows)
        imaginary_rows = expand_rows(real_full, sine_rows) + expand_rows(
            imaginary_full, cosine_rows
        )
        stacked = jnp.concatenate([real_rows, imaginary_rows], axis=-1).reshape(
            planes_here * channels * local_rows, 2 * MY
        )
        spectral = jnp.dot(stacked, inverse_cols, precision=highest)
        layer_spectral = spectral.reshape(planes_here, channels, local_rows, local_cols)
        padded = padded_2(planes_block, (("gx", 2), ("gy", 3)), 4)
        exponents = jnp.exp(mix_logits[layer_index])
        mixture = exponents / jnp.sum(exponents)
        bias_column = channel_bias[layer_index][:, None, None]
        row_pieces = []
        for block_index in range(row_blocks):
            first_row = block_index * block_rows
            near_term = conv_rows(
                padded[0], conv_near[layer_index], 1, 3, first_row, block_rows, local_cols
            )
            far_term = conv_rows(
                padded[0], conv_far[layer_index], 2, 5, first_row, block_rows, local_cols
            )
            spectral_rows = layer_spectral[0, :, first_row : first_row + block_rows, :]
            summed = (
                mixture[0] * spectral_rows
                + mixture[1] * near_term
                + mixture[2] * far_term
                + bias_column
            )
            row_pieces.append(jax.nn.gelu(summed, approximate=False).astype(jnp.bfloat16))
        outputs = [jnp.concatenate(row_pieces, axis=1)]
        planes_block = jnp.stack(outputs)
    return planes_block


def solution(mesh):
    in_specs = (
        P(None, None, "gx", "gy"),
        P(None, None, None, None, ("gx", "gy")),
        P(),
        P(),
        P(),
        P(),
    )
    out_specs = P(None, None, "gx", "gy")
    return jax.shard_map(
        on_device, mesh=mesh, in_specs=in_specs, out_specs=out_specs, check_vma=False
    )
```

profile of v0, /device:TPU:0, one launch (start us, length us, event | category | flops | bytes accessed | tf_op | source)
XLA Modules:
  0.0 1025.7 jit_solution(15079216024907753427)
XLA Ops:
  8.8 6.0 collective-permute-start.1
  37.3 2.9 collective-permute-start.3
  71.0 3.8 copy-done.15
  74.8 14.7 %constant_dynamic-update-slice_fusion.20 = (bf16[25,20,32,256]{3,1,2,0:T(8,128)(2,1)}, bf16[25,20,32,256]{3,1,2,0:T(8,128)(2,1)S(1)}, bf16[9,20,32,256]{3,1,2,0:...) fusion(bf16[25,20,32,256]{3,1,2,0:T(8,128)(2,1)} %get-tuple-ele, ...), kind=kLoop, calls=%fused_computation.275 | loop fusion | bytes 5505024
  106.9 2.4 convolution_bitcast_fusion.5
  109.3 6.5 convolution_bitcast_fusion.7
  124.9 39.9 %all-reduce.3.cloned.1.call-done = f32[2,1,20,2048]{3,0,2,1:T(2,128)} async-done(((f32[2,1,20,2048]{3,0,2,1:T(2,128)}), f32[2,1,20,2048]{3,0,2,1:T(2,128)}) %all-reduce.3.cloned.1.call-update) | async-done | bytes 327696 | tf_op jit(solution)/shard_map/psum | solution.py:113
  167.1 326.2 %all-gather = f32[256,1,20,16]{2,3,1,0:T(8,128)S(1)} all-gather(f32[2,1,20,16]{2,3,1,0:T(8,128)S(1)} %pad_maximum_fusion.8), channel_id=2, replica_groups=mesh['gx'=16,'gy'=8] {'gx','gy'}, dimensions={0}, use_global_device_ids=true | all-gather | bytes 330240 | tf_op jit(solution)/shard_map/all_gather | solution.py:128
  503.2 10.4 %fusion.42 = (bf16[20,32,256]{2,1,0:T(8,128)(2,1)S(1)}, bf16[20,32,256]{2,1,0:T(8,128)(2,1)S(1)}, bf16[20,32,256]{2,1,0:T(8,128)(2,1)S(1)}, bf16[20,32,256]{2,1,0:T(8,128)(2,1)S(1)}) fusion(f32[32,256,20]{1,2,0:T(8,128)} %convolution_bitcast_fusion.9, f32[32,256,20]{1,2,0:T(8,128)} %convolution_bitcast_fusion.10, ...), kind=kLoop, calls=%fused_computation.51 | loop fusion | flops 46530560 | bytes 9175132 | tf_op jit(solution)/shard_map/convert_element_type | solution.py:165
  516.9 5.3 collective-permute-start.5
  526.1 4.3 collective-permute-start.7
  548.7 3.2 copy-done.18
  554.4 2.9 constant_dynamic-update-slice_fusion.146
  557.2 2.7 constant_dynamic-update-slice_fusion.145
  560.0 2.6 constant_dynamic-update-slice_fusion.144
  562.6 2.9 constant_dynamic-update-slice_fusion.143
  565.5 2.6 constant_dynamic-update-slice_fusion.142
  568.1 2.6 constant_dynamic-update-slice_fusion.141
  570.7 2.6 constant_dynamic-update-slice_fusion.140
  573.2 2.5 constant_dynamic-update-slice_fusion.139
  576.2 2.8 copy-done.16
  579.2 4.5 fusion.25
  583.7 9.6 fusion.19
  593.3 5.3 fusion.22
  598.6 5.3 fusion.16
  603.8 2.6 fusion.28
  606.4 2.8 fusion.31
  609.2 2.6 fusion.34
  611.7 2.6 fusion.37
  614.3 58.0 %all-reduce.5.cloned.1.call-done = f32[2,1,20,2048]{3,0,2,1:T(2,128)} async-done(((f32[2,1,20,2048]{3,0,2,1:T(2,128)}), f32[2,1,20,2048]{3,0,2,1:T(2,128)}) %all-reduce.5.cloned.1.call-update) | async-done | bytes 327696 | tf_op jit(solution)/shard_map/psum | solution.py:113
  674.7 325.8 %all-gather.1 = f32[256,1,20,16]{2,3,1,0:T(8,128)S(1)} all-gather(f32[2,1,20,16]{2,3,1,0:T(8,128)S(1)} %pad_maximum_fusion.9), channel_id=3, replica_groups=mesh['gx'=16,'gy'=8] {'gx','gy'}, dimensions={0}, use_global_device_ids=true | all-gather | bytes 330240 | tf_op jit(solution)/shard_map/all_gather | solution.py:128
  1006.8 10.5 %fusion.54 = (bf16[20,32,256]{2,1,0:T(8,128)(2,1)S(1)}, bf16[20,32,256]{2,1,0:T(8,128)(2,1)S(1)}, bf16[20,32,256]{2,1,0:T(8,128)(2,1)S(1)}, bf16[20,32,256]{2,1,0:T(8,128)(2,1)S(1)}) fusion(f32[32,256,20]{1,2,0:T(8,128)} %fusion.16, f32[32,256,20]{1,2,0:T(8,128)} %fusion.28, f32[1,20,128,256]{3,2,1,0:T(8,128)S(1)} %convolution_bitcast_fusion.1, ...), kind=kLoop, calls=%fused_computation.63 | loop fusion | flops 46530560 | bytes 9175132 | tf_op jit(solution)/shard_map/convert_element_type | solution.py:165
  (241 shorter events, 131.9 us)
Async XLA Ops:
  6.5 15.6 %copy-start.8 = (bf16[2,20,500]{2,0,1:T(2,128)(2,1)S(1)}, bf16[2,20,500]{2,0,1:T(2,128)(2,1)}, u32[]{:S(2)}) copy-start(bf16[2,20,500]{2,0,1:T(2,128)(2,1)} %param.9) | copy-start | bytes 120004
  6.5 158.2 %all-reduce.3.cloned.1.call-start = ((), (), s32[]{:S(2)}) async-start(), calls=%async_computation | async-start | bytes 655360 | tf_op jit(solution)/shard_map/psum | solution.py:113
  8.1 23.0 %collective-permute-start = (bf16[1,20,4,256]{3,1,2,0:T(8,128)(2,1)}, bf16[1,20,4,256]{3,1,2,0:T(8,128)(2,1)}, u32[]{:S(2)}, u32[]{:S(2)}) collective-permute-start(bf16[1,20,4,256]{3,1,2,0:T(8,128)(2,1)} %copy.500), channel_id=1, source_target_pairs={{0,8},{8,16},{16,24},{24,32},{32,40},{40,48},{48,56},{56,64},{64,7... | collective-permute-start | bytes 122888 | tf_op jit(solution)/shard_map/ppermute | solution.py:25
  8.8 24.0 %collective-permute-start.1 = (bf16[1,20,4,256]{3,1,2,0:T(8,128)(2,1)}, bf16[1,20,4,256]{3,1,2,0:T(8,128)(2,1)}, u32[]{:S(2)}, u32[]{:S(2)}) collective-permute-start(bf16[1,20,4,256]{3,1,2,0:T(8,128)(2,1)} %copy.501), channel_id=1, source_target_pairs={{8,0},{16,8},{24,16},{32,24},{40,32},{48,40},{56,48},{64,56},{72,6... | collective-permute-start | bytes 122888 | tf_op jit(solution)/shard_map/ppermute | solution.py:26
  15.0 7.2 copy-start.11
  15.0 7.2 copy-start.13
  15.0 10.7 %copy-start.19 = (f32[2,3]{1,0:T(2,128)S(1)}, f32[2,3]{1,0:T(2,128)}, u32[]{:S(2)}) copy-start(f32[2,3]{1,0:T(2,128)} %param.10) | copy-start | bytes 76
  15.0 17.0 %copy-start = (bf16[1,20,128,256]{3,2,1,0:T(8,128)(2,1)S(1)}, bf16[1,20,128,256]{3,2,1,0:T(8,128)(2,1)}, u32[]{:S(2)}) copy-start(bf16[1,20,128,256]{3,2,1,0:T(8,128)(2,1)} %param.6) | copy-start | bytes 3932164
  22.1 650.2 %all-reduce.5.cloned.1.call-start = ((), (), s32[]{:S(2)}) async-start(), calls=%async_computation.1 | async-start | bytes 655360 | tf_op jit(solution)/shard_map/psum | solution.py:113
  35.1 12.2 %collective-permute-start.2 = (bf16[1,20,136,4]{2,3,1,0:T(4,128)(2,1)}, bf16[1,20,136,4]{2,3,1,0:T(4,128)(2,1)S(1)}, u32[]{:S(2)}, u32[]{:S(2)}) collective-permute-start(bf16[1,20,136,4]{2,3,1,0:T(4,128)(2,1)} %copy.211), channel_id=1, source_target_pairs={{0,1},{1,2},{2,3},{3,4},{4,5},{5,6},{6,7},{7,0},{8,9},{9,10},{10,1... | collective-permute-start | bytes 65288 | tf_op jit(solution)/shard_map/ppermute | solution.py:25
  37.3 10.6 %collective-permute-start.3 = (bf16[1,20,136,4]{2,3,1,0:T(4,128)(2,1)S(1)}, bf16[1,20,136,4]{2,3,1,0:T(4,128)(2,1)}, u32[]{:S(2)}, u32[]{:S(2)}) collective-permute-start(bf16[1,20,136,4]{2,3,1,0:T(4,128)(2,1)S(1)} %copy.212), channel_id=1, source_target_pairs={{1,0},{2,1},{3,2},{4,3},{5,4},{6,5},{7,6},{0,7},{9,8},{10,9},{11,1... | collective-permute-start | bytes 65288 | tf_op jit(solution)/shard_map/ppermute | solution.py:26
  71.0 3.8 copy-start.15
  100.3 4.3 copy-start.7
  106.9 8.9 slice-start
  106.9 8.9 slice-start.1
  109.3 6.5 slice-start.2
  120.4 45.4 %copy-start.4 = (f32[20,20,16]{1,2,0:T(8,128)S(1)}, f32[20,20,16]{1,2,0:T(8,128)}, u32[]{:S(2)}) copy-start(f32[20,20,16]{1,2,0:T(8,128)} %get-tuple-element.287) | copy-start | bytes 76804
  120.4 46.1 %copy-start.3 = (f32[20,20,16]{1,2,0:T(8,128)S(1)}, f32[20,20,16]{1,2,0:T(8,128)}, u32[]{:S(2)}) copy-start(f32[20,20,16]{1,2,0:T(8,128)} %get-tuple-element.286) | copy-start | bytes 76804
  124.9 376.1 %copy-start.6 = (f32[32,256]{1,0:T(8,128)S(1)}, f32[32,256]{1,0:T(8,128)}, u32[]{:S(2)}) copy-start(f32[32,256]{1,0:T(8,128)} %get-tuple-element.296) | copy-start | bytes 98308
  167.1 336.1 %copy-start.21 = (f32[20]{0:T(128)S(1)}, f32[20]{0:T(128)}, u32[]{:S(2)}) copy-start(f32[20]{0:T(128)} %get-tuple-element.300) | copy-start | bytes 244
  494.2 9.0 copy-start.1
  500.9 12.8 %copy-start.12 = (bf16[256,32]{0,1:T(8,128)(2,1)S(1)}, bf16[256,32]{0,1:T(8,128)(2,1)}, u32[]{:S(2)}) copy-start(bf16[256,32]{0,1:T(8,128)(2,1)} %copy-done.11) | copy-start | bytes 49156
  500.9 12.8 %copy-start.14 = (bf16[256,32]{0,1:T(8,128)(2,1)S(1)}, bf16[256,32]{0,1:T(8,128)(2,1)}, u32[]{:S(2)}) copy-start(bf16[256,32]{0,1:T(8,128)(2,1)} %copy-done.13) | copy-start | bytes 49156
  516.8 7.1 collective-permute-start.4
  516.9 7.0 collective-permute-start.5
  525.6 6.2 collective-permute-start.6
  526.1 6.0 collective-permute-start.7
  568.1 11.1 %copy-start.9 = (bf16[20,25,20]{1,0,2:T(8,128)(2,1)S(1)}, bf16[20,25,20]{1,0,2:T(8,128)(2,1)}, u32[]{:S(2)}) copy-start(bf16[20,25,20]{1,0,2:T(8,128)(2,1)} %copy.257) | copy-start | bytes 60004
  583.7 9.6 copy-start.17
  598.6 5.3 copy-start.10
  606.4 66.9 %copy-start.2 = (f32[20,20,16]{1,2,0:T(8,128)S(1)}, f32[20,20,16]{1,2,0:T(8,128)}, u32[]{:S(2)}) copy-start(f32[20,20,16]{1,2,0:T(8,128)} %get-tuple-element.285) | copy-start | bytes 76804
  674.7 332.2 %copy-start.20 = (f32[20]{0:T(128)S(1)}, f32[20]{0:T(128)}, u32[]{:S(2)}) copy-start(f32[20]{0:T(128)} %get-tuple-element.299) | copy-start | bytes 244
  (3 other events, 8.9 us)
Sparse Core Ops, SparseCore 0:
  22.2 142.4 all-reduce.2
  531.7 140.5 all-reduce.4
where the time goes:
time: 1030 us
  blocking collectives  652 us (63%)
  local copies, waits for them, and re-layouts  131 us (13%)
  waiting for transfers between devices  98.6 us (10%)
  matrix products  74.6 us (7%)
  other arithmetic  34.5 us (3%)
  starting transfers between devices  20.3 us (2%)
  between operations  14.7 us (1%)
    all_gather x2, blocking collectives, on_device(): gathered = lax.all_gather(own_block, ('gx', 'gy'), axis=0, tiled=True)  652 us
    unnamed x121, local copies, waits for them, and re-layouts  98.1 us
    psum x2, waiting for transfers between devices, on_device(): totals = lax.psum(partial_value, ('gx', 'gy'))  97.8 us
    dot_general x16, matrix products, conv_rows(): jnp.einsum('otc,tcxy->oxy', shaped_weights, stacked, preferred_element_ty...  53.9 us
    convert_element_type x2, other arithmetic, on_device(): jax.nn.gelu(summed, approximate=False).astype(jnp.bfloat16)  20.9 us
  transfers between devices with their start and end apart: 10, of which 4 were waited for; matrix products, arithmetic and copies ran while one was open for 18% of the time, Pallas kernels for 0%

commit v1 on v0

--- a/solution.py
+++ b/solution.py
@@ -110,7 +110,9 @@
                 imaginary_spec.reshape(planes_here, channels, MODES),
             ]
         )
-        totals = lax.psum(partial_value, ("gx", "gy"))
+        totals = partial_value
+        for mesh_axis in ("gy", "gx"):
+            totals = lax.psum(totals, mesh_axis)
         own_modes = lax.dynamic_slice_in_dim(totals, mode_start, share_modes, 3)
 
         def mix_modes(spectrum, weights):

time: 1030 us -> 1200 us (1.17)
  waiting for transfers between devices: 98.6 us -> 259 us
    psum x2 -> x4, waiting for transfers between devices: 97.8 us -> 258 us  [on_device(): totals = lax.psum(totals, mesh_axis)]
  transfers between devices with their start and end apart: 10 -> 12, of which waited for: 4 -> 4; matrix products, arithmetic and copies ran while one was open for 18% -> 15% of each run, Pallas kernels for 0% -> 0%
where the time goes in v1:
time: 1200 us
  blocking collectives  654 us (54%)
  waiting for transfers between devices  259 us (22%)
  local copies, waits for them, and re-layouts  131 us (11%)
  matrix products  82.2 us (7%)
  other arithmetic  35.4 us (3%)
  starting transfers between devices  20.5 us (2%)
  between operations  14.4 us (1%)
    all_gather x2, blocking collectives, on_device(): gathered = lax.all_gather(own_block, ('gx', 'gy'), axis=0, tiled=True)  654 us
    psum x4, waiting for transfers between devices, on_device(): totals = lax.psum(totals, mesh_axis)  258 us
    unnamed x121, local copies, waits for them, and re-layouts  105 us
    dot_general x16, matrix products, conv_rows(): jnp.einsum('otc,tcxy->oxy', shaped_weights, stacked, preferred_element_ty...  57.8 us
  transfers between devices with their start and end apart: 12, of which 4 were waited for; matrix products, arithmetic and copies ran while one was open for 15% of the time, Pallas kernels for 0%

profile of v1, /device:TPU:0, one launch (start us, length us, event | category | flops | bytes accessed | tf_op | source)
XLA Modules:
  0.0 1197.0 jit_solution(9901035470361813154)
XLA Ops:
  8.8 6.0 collective-permute-start.1
  32.4 2.9 collective-permute-start.3
  41.6 3.2 maximum_bitcast_fusion
  65.8 3.8 copy-done.16
  69.6 14.6 %constant_dynamic-update-slice_fusion.20 = (bf16[25,20,32,256]{3,1,2,0:T(8,128)(2,1)}, bf16[25,20,32,256]{3,1,2,0:T(8,128)(2,1)S(1)}, bf16[9,20,32,256]{3,1,2,0:...) fusion(bf16[25,20,32,256]{3,1,2,0:T(8,128)(2,1)} %get-tuple-ele, ...), kind=kLoop, calls=%fused_computation.275 | loop fusion | bytes 5505024
  104.2 6.4 convolution_bitcast_fusion.7
  124.5 3.5 convolution_bitcast_fusion.10
  128.0 127.9 %all-reduce.7.cloned.1.call-done = f32[2,1,20,2048]{3,0,2,1:T(2,128)} async-done(((f32[2,1,20,2048]{3,0,2,1:T(2,128)}), f32[2,1,20,2048]{3,0,2,1:T(2,128)}) %all-reduce.7.cloned.1.call-update) | async-done | bytes 327696 | tf_op jit(solution)/shard_map/psum | solution.py:115
  262.0 327.5 %all-gather = f32[256,1,20,16]{2,3,1,0:T(8,128)S(1)} all-gather(f32[2,1,20,16]{2,3,1,0:T(8,128)S(1)} %pad_maximum_fusion.8), channel_id=2, replica_groups=mesh['gx'=16,'gy'=8] {'gx','gy'}, dimensions={0}, use_global_device_ids=true | all-gather | bytes 330240 | tf_op jit(solution)/shard_map/all_gather | solution.py:130
  599.3 10.3 fusion.42
  612.9 5.3 collective-permute-start.5
  622.2 4.2 collective-permute-start.7
  644.8 3.2 copy-done.19
  650.4 2.9 constant_dynamic-update-slice_fusion.146
  653.3 2.7 constant_dynamic-update-slice_fusion.145
  656.0 2.6 constant_dynamic-update-slice_fusion.144
  658.7 2.9 constant_dynamic-update-slice_fusion.143
  661.6 2.6 constant_dynamic-update-slice_fusion.142
  664.2 2.6 constant_dynamic-update-slice_fusion.141
  666.7 2.6 constant_dynamic-update-slice_fusion.140
  672.3 2.8 copy-done.17
  675.2 4.5 fusion.25
  679.8 9.6 fusion.19
  689.4 5.3 fusion.22
  694.6 5.3 fusion.16
  699.9 2.6 fusion.28
  702.5 2.8 fusion.31
  705.2 2.6 fusion.34
  707.8 4.4 fusion.37
  712.2 130.4 %all-reduce.11.cloned.1.call-done = f32[2,1,20,2048]{3,0,2,1:T(2,128)} async-done(((f32[2,1,20,2048]{3,0,2,1:T(2,128)}), f32[2,1,20,2048]{3,0,2,1:T(2,128)}) %all-reduce.11.cloned.1.call-update) | async-done | bytes 327696 | tf_op jit(solution)/shard_map/psum | solution.py:115
  845.1 327.0 %all-gather.1 = f32[256,1,20,16]{2,3,1,0:T(8,128)S(1)} all-gather(f32[2,1,20,16]{2,3,1,0:T(8,128)S(1)} %pad_maximum_fusion.9), channel_id=3, replica_groups=mesh['gx'=16,'gy'=8] {'gx','gy'}, dimensions={0}, use_global_device_ids=true | all-gather | bytes 330240 | tf_op jit(solution)/shard_map/all_gather | solution.py:130
  1178.4 10.5 fusion.54
  (247 shorter events, 137.1 us)
Async XLA Ops:
  6.5 15.7 %copy-start.7 = (bf16[2,20,500]{2,0,1:T(2,128)(2,1)S(1)}, bf16[2,20,500]{2,0,1:T(2,128)(2,1)}, u32[]{:S(2)}) copy-start(bf16[2,20,500]{2,0,1:T(2,128)(2,1)} %param.9) | copy-start | bytes 120004
  6.5 117.0 %all-reduce.5.cloned.1.call-start = ((), (), s32[]{:S(2)}) async-start(), calls=%async_computation | async-start | bytes 655360 | tf_op jit(solution)/shard_map/psum | solution.py:115
  8.1 19.1 %collective-permute-start = (bf16[1,20,4,256]{3,1,2,0:T(8,128)(2,1)}, bf16[1,20,4,256]{3,1,2,0:T(8,128)(2,1)S(1)}, u32[]{:S(2)}, u32[]{:S(2)}) collective-permute-start(bf16[1,20,4,256]{3,1,2,0:T(8,128)(2,1)} %copy.500), channel_id=1, source_target_pairs={{0,8},{8,16},{16,24},{24,32},{32,40},{40,48},{48,56},{56,64},{64,7... | collective-permute-start | bytes 122888 | tf_op jit(solution)/shard_map/ppermute | solution.py:25
  8.8 19.2 %collective-permute-start.1 = (bf16[1,20,4,256]{3,1,2,0:T(8,128)(2,1)}, bf16[1,20,4,256]{3,1,2,0:T(8,128)(2,1)S(1)}, u32[]{:S(2)}, u32[]{:S(2)}) collective-permute-start(bf16[1,20,4,256]{3,1,2,0:T(8,128)(2,1)} %copy.501), channel_id=1, source_target_pairs={{8,0},{16,8},{24,16},{32,24},{40,32},{48,40},{56,48},{64,56},{72,6... | collective-permute-start | bytes 122888 | tf_op jit(solution)/shard_map/ppermute | solution.py:26
  15.0 7.2 copy-start.11
  15.0 7.2 copy-start.13
  15.0 10.1 copy-start.20
  15.0 10.8 copy-start.21
  15.0 12.1 %copy-start.10 = (bf16[2,20,180]{2,0,1:T(2,128)(2,1)S(1)}, bf16[2,20,180]{2,0,1:T(2,128)(2,1)}, u32[]{:S(2)}) copy-start(bf16[2,20,180]{2,0,1:T(2,128)(2,1)} %param.8) | copy-start | bytes 43204
  15.0 12.2 %copy-start.1 = (bf16[1,20,128,256]{3,2,1,0:T(8,128)(2,1)S(1)}, bf16[1,20,128,256]{3,2,1,0:T(8,128)(2,1)}, u32[]{:S(2)}) copy-start(bf16[1,20,128,256]{3,2,1,0:T(8,128)(2,1)} %param.6) | copy-start | bytes 3932164
  22.1 233.8 %all-reduce.7.cloned.1.call-start = ((), (), s32[]{:S(2)}) async-start(), calls=%async_computation.1 | async-start | bytes 655360 | tf_op jit(solution)/shard_map/psum | solution.py:115
  30.2 9.5 collective-permute-start.2
  32.4 7.8 collective-permute-start.3
  95.1 4.3 copy-start.6
  101.7 8.9 slice-start
  101.7 8.9 slice-start.1
  104.2 6.4 slice-start.2
  123.5 584.3 %all-reduce.9.cloned.1.call-start = ((), (), s32[]{:S(2)}) async-start(), calls=%async_computation.2 | async-start | bytes 655360 | tf_op jit(solution)/shard_map/psum | solution.py:115
  128.0 469.0 %copy-start.5 = (f32[32,256]{1,0:T(8,128)S(1)}, f32[32,256]{1,0:T(8,128)}, u32[]{:S(2)}) copy-start(f32[32,256]{1,0:T(8,128)} %get-tuple-element.296) | copy-start | bytes 98308
  590.4 9.0 copy-start.2
  597.0 12.7 %copy-start.12 = (bf16[256,32]{0,1:T(8,128)(2,1)S(1)}, bf16[256,32]{0,1:T(8,128)(2,1)}, u32[]{:S(2)}) copy-start(bf16[256,32]{0,1:T(8,128)(2,1)} %copy-done.11) | copy-start | bytes 49156
  597.1 12.7 %copy-start.14 = (bf16[256,32]{0,1:T(8,128)(2,1)S(1)}, bf16[256,32]{0,1:T(8,128)(2,1)}, u32[]{:S(2)}) copy-start(bf16[256,32]{0,1:T(8,128)(2,1)} %copy-done.13) | copy-start | bytes 49156
  612.9 7.1 collective-permute-start.4
  612.9 7.0 collective-permute-start.5
  621.7 6.2 collective-permute-start.6
  622.2 6.0 collective-permute-start.7
  627.4 215.2 %all-reduce.11.cloned.1.call-start = ((), (), s32[]{:S(2)}) async-start(), calls=%async_computation.3 | async-start | bytes 655360 | tf_op jit(solution)/shard_map/psum | solution.py:115
  664.2 11.1 copy-start.8
  671.8 8.0 copy-start.15
  679.8 9.6 copy-start.18
  694.6 5.3 copy-start.9
  702.5 141.3 %copy-start.3 = (f32[20,20,16]{1,2,0:T(8,128)S(1)}, f32[20,20,16]{1,2,0:T(8,128)}, u32[]{:S(2)}) copy-start(f32[20,20,16]{1,2,0:T(8,128)} %get-tuple-element.285) | copy-start | bytes 76804
  (5 other events, 13.9 us)
Sparse Core Ops, SparseCore 0:
  22.2 73.9 all-reduce.4
  123.6 132.2 all-reduce.6
  627.6 72.3 all-reduce.8
  707.9 134.6 all-reduce.10
